TPU v7x, 32 devices: a whole 2x2x4 slice. The times are simulated.
32 devices in a mesh: tile: 16 (over z, y, x), day: 2 (over core).
Axes of the slice: x: 2, y: 2, z: 4, core: 2. Of those that a mesh axis runs over, the one named last changes fastest.
Arguments:
- spectra: bfloat16 [2, 4096, 2, 4, 512], P('day', 'tile'), may hold values from -500 to 500
- band_low: int32 [32], P('tile'), may hold values from 0 to 127
- band_high: int32 [32], P('tile'), may hold values from 384 to 512
- pair_list: int32 [64, 2], P('tile'), may hold values from -1 to 31, as said below
Outputs:
- correlations: float32 [2, 64, 128, 128], P('day', 'tile')
Inputs may be any that keep to these rules, and one draw needn't show every extreme that they name: `pair_list`: row p is either a pair (a, b) with 2 * (p // 4) <= a < 2 * (p // 4) + 2 and 0 <= b - a <= 6, or (-1, -1). In each aligned run of 4 rows the pairs come first, there is at least one, and in every draw some run holds 4 pairs.
All inputs are finite; a program needn't handle non-finite values.
Results may differ from a plain program's by a relative error of at most 0.0027.
Values may be sent and summed in bfloat16 or wider, within the bound.
A program may use at most 128 MiB of HBM per device.

v0:
```python
import functools
import math

import jax
import jax.numpy as jnp
import numpy as np
from jax import lax
from jax.experimental import pallas as pl
from jax.experimental.pallas import tpu as pltpu
from jax.sharding import PartitionSpec as P

BLK_DEV = 2
SEGLEN = 15000
FIRST = 90
HALF_WIN = 64
LSTEP = 25
REACH = 3
BELOW = 1
MESH = pl.DeviceIdType.MESH
VMEM = pl.BlockSpec(memory_space=pltpu.VMEM)
SMEM = pl.BlockSpec(memory_space=pltpu.SMEM)


def phase_tables(lag_total, bin_count):
    lag_samples = (np.arange(lag_total) - lag_total // 2) * LSTEP
    bin_number = FIRST + np.arange(bin_count)
    phase_turns = lag_samples[:, None] * bin_number[None, :] % SEGLEN
    phase_angle = phase_turns.astype(np.float32) * np.float32(2.0 * math.pi / SEGLEN)
    return np.stack([np.cos(phase_angle), np.sin(phase_angle)], axis=1).astype(np.float32)


def mixed(index, offset):
    result = index
    bit = 1
    while bit <= offset:
        if offset & bit:
            result = result + bit - 2 * bit * ((index // bit) % 2)
        bit *= 2
    return result


def correlate_kernel(
    tiles, days, group, norm_factor, low_ref, high_ref, own_pair_ref, trig_ref, raw_hbm, out_ref,
    raw_ref, raw_sem, own_ref, spread_ref, win_ref, gath_ref, pair_ref,
    rot_ref, part_ref, day_buf, send_buf, recv_buf, top_buf, down_src, down_buf,
    send_sem, recv_sem, far_send, far_recv, pair_send, pair_recv, up_send, up_recv, own_sem,
    day_send, day_recv, tile_send, tile_recv, top_send, top_recv, down_send, down_recv,
):
    here = lax.axis_index("tile")
    day = lax.axis_index("day")
    spot = here % group
    base = here - spot
    chunks = 2 * BLK_DEV
    has_below = base > 0
    has_above = base + group < tiles
    upper = REACH - BELOW

    last = group - 1
    turns = list(range(1, last)) + [0, last]
    items = [(offset, block) for block in range(BLK_DEV) for offset in turns]

    def fetch(offset, block):
        there = mixed(spot, offset)
        return pltpu.make_async_copy(
            raw_hbm.at[there, :, block], raw_ref.at[there, :, block], raw_sem.at[offset, block]
        )

    for item in items:
        fetch(*item).start()
    is_top = base + group == tiles
    base_block = (base - BELOW) * BLK_DEV
    window_tiles, _, _, chans, _ = win_ref.shape
    lags = days
    rows_dev = out_ref.shape[1]

    barrier = pltpu.get_barrier_semaphore()
    for offset in range(1, days):
        pl.semaphore_signal(
            barrier, inc=1, device_id={"day": (day + offset) % days}, device_id_type=MESH
        )
    for offset in range(1, group):
        pl.semaphore_signal(
            barrier, inc=1, device_id={"tile": base + mixed(spot, offset)}, device_id_type=MESH
        )

    @pl.when(has_below)
    def _():
        pl.semaphore_signal(barrier, inc=1, device_id={"tile": here - group}, device_id_type=MESH)

    @pl.when(has_above)
    def _():
        pl.semaphore_signal(barrier, inc=1, device_id={"tile": here + group}, device_id_type=MESH)

    bins = raw_ref.shape[-1]
    row = lax.broadcasted_iota(jnp.int32, (bins, bins), 0)
    col = lax.broadcasted_iota(jnp.int32, (bins, bins), 1)
    spread_ref[...] = jnp.where(jnp.abs(row - col) <= HALF_WIN, 1.0, 0.0).astype(jnp.bfloat16)
    bin_index = lax.broadcasted_iota(jnp.int32, (1, bins), 1)
    counts = (
        jnp.minimum(bin_index + HALF_WIN, bins - 1) - jnp.maximum(bin_index - HALF_WIN, 0) + 1
    ).astype(jnp.float32)
    gath_ref[BELOW + spot, 0:2, 0:rows_dev] = own_pair_ref[...]

    @pl.when(base == 0)
    def _():
        gath_ref[0] = jnp.full(gath_ref.shape[1:], -1, jnp.int32)

    peers = days - 1 + group - 1 + has_below.astype(jnp.int32) + has_above.astype(jnp.int32)
    pl.semaphore_wait(barrier, peers)

    def whiten(there, block):
        real = raw_ref[there, 0, block].astype(jnp.float32)
        imag = raw_ref[there, 1, block].astype(jnp.float32)
        magnitude = jnp.sqrt(real * real + imag * imag)
        coarse = magnitude.astype(jnp.bfloat16)
        fine = (magnitude - coarse.astype(jnp.float32)).astype(jnp.bfloat16)
        spread = spread_ref[...]
        sums = jnp.dot(coarse, spread, preferred_element_type=jnp.float32) + jnp.dot(
            fine, spread, preferred_element_type=jnp.float32
        )
        amplitude = sums / counts + 1e-05
        keep = (bin_index >= low_ref[block]) & (bin_index < high_ref[block])
        gain = 1.0 / amplitude
        own_ref[there, 0, block] = jnp.where(keep, real * gain, 0.0).astype(jnp.bfloat16)
        own_ref[there, 1, block] = jnp.where(keep, imag * gain, 0.0).astype(jnp.bfloat16)

    def across(offset, chunk):
        block, part = divmod(chunk, 2)
        there = mixed(spot, offset)
        return pltpu.make_async_remote_copy(
            src_ref=own_ref.at[there, part, block],
            dst_ref=win_ref.at[BELOW + spot, part, block],
            send_sem=send_sem.at[offset - 1, chunk],
            recv_sem=recv_sem.at[offset - 1, chunk],
            device_id={"tile": base + there},
            device_id_type=MESH,
        )

    def pairs_across(offset):
        return pltpu.make_async_remote_copy(
            src_ref=gath_ref.at[BELOW + spot],
            dst_ref=gath_ref.at[BELOW + spot],
            send_sem=pair_send.at[offset - 1],
            recv_sem=pair_recv.at[offset - 1],
            device_id={"tile": base + mixed(spot, offset)},
            device_id_type=MESH,
        )

    def pairs_up():
        return pltpu.make_async_remote_copy(
            src_ref=gath_ref.at[group],
            dst_ref=gath_ref.at[0],
            send_sem=up_send,
            recv_sem=up_recv,
            device_id={"tile": here + group},
            device_id_type=MESH,
        )

    def far(source, slot, target, device, chunk):
        block, part = divmod(chunk, 2)
        index = 0 if target == 0 else target - BELOW - group + 1
        return pltpu.make_async_remote_copy(
            src_ref=source.at[slot, part, block],
            dst_ref=win_ref.at[target, part, block],
            send_sem=far_send.at[index, chunk],
            recv_sem=far_recv.at[index, chunk],
            device_id={"tile": device},
            device_id_type=MESH,
        )

    def relay(source, slot, where, chunk_list):
        for lower in range(upper):

            @pl.when(has_below & (where == lower))
            def _():
                for chunk in chunk_list:
                    far(source, slot, BELOW + group + lower, here - group, chunk).start()

        @pl.when(has_above & (where == group - 1))
        def _():
            for chunk in chunk_list:
                far(source, slot, 0, here + group, chunk).start()

    def send(offset, block):
        if offset:
            for part in range(2):
                across(offset, 2 * block + part).start()
        else:
            relay(own_ref, spot, spot, [2 * block, 2 * block + 1])

    for index, (offset, block) in enumerate(items):
        fetch(offset, block).wait()
        whiten(mixed(spot, offset), block)
        if index:
            send(*items[index - 1])
        else:
            for peer in range(1, group):
                pairs_across(peer).start()
    send(*items[-1])
    stay = pltpu.make_async_copy(own_ref.at[spot], win_ref.at[BELOW + spot], own_sem)
    stay.start()

    for chunk in range(chunks):
        for offset in range(1, group):
            across(offset, chunk).wait_recv()
            there = mixed(spot, offset)
            relay(win_ref, BELOW + there, there, [chunk])

    def rotate(tile, carry):
        for block in range(BLK_DEV):
            real = win_ref[tile, 0, block].astype(jnp.float32)
            imag = win_ref[tile, 1, block].astype(jnp.float32)
            for lag in range(lags):
                cosine = trig_ref[lag, 0:1]
                sine = trig_ref[lag, 1:2]
                rows = slice(lag * chans, (lag + 1) * chans)
                rot_ref[tile * BLK_DEV + block, 0, rows] = (real * cosine + imag * sine).astype(
                    jnp.bfloat16
                )
                rot_ref[tile * BLK_DEV + block, 1, rows] = (imag * cosine - real * sine).astype(
                    jnp.bfloat16
                )
        return carry

    for chunk in range(chunks):
        for offset in range(1, group):
            across(offset, chunk).wait_send()
    stay.wait()
    for offset in range(1, group):
        pairs_across(offset).wait()

    @pl.when(has_above)
    def _():
        pairs_up().start()

    lax.fori_loop(BELOW, BELOW + group, rotate, 0)

    @pl.when(has_above)
    def _():
        pairs_up().wait_send()
        for chunk in range(chunks):
            far(own_ref, 0, 0, here + group, chunk).wait_send()
            for lower in range(upper):
                far(own_ref, 0, BELOW + group + lower, here, chunk).wait_recv()

    @pl.when(has_below)
    def _():
        pairs_up().wait_recv()
        for chunk in range(chunks):
            far(own_ref, 0, 0, here, chunk).wait_recv()
            for lower in range(upper):
                far(own_ref, 0, BELOW + group + lower, here - group, chunk).wait_send()

    gather_pairs = pltpu.make_async_copy(gath_ref, pair_ref, own_sem)
    gather_pairs.start()
    lax.fori_loop(0, BELOW, rotate, 0)
    lax.fori_loop(BELOW + group, window_tiles, rotate, 0)
    gather_pairs.wait()

    def products(set_index, slot):
        for row in range(rows_dev):
            first = pair_ref[set_index, 0, row]
            second = pair_ref[set_index, 1, row]
            left = jnp.clip(first - base_block, 0, window_tiles * BLK_DEV - 1)
            right = jnp.clip(second - base_block, 0, window_tiles * BLK_DEV - 1)
            total = jnp.zeros((chans, lags * chans), jnp.float32)
            for part in range(2):
                total = total + lax.dot_general(
                    win_ref[left // BLK_DEV, part, left % BLK_DEV],
                    rot_ref[right, part],
                    (((1,), (1,)), ((), ())),
                    preferred_element_type=jnp.float32,
                )
            total = jnp.where(first >= 0, total * norm_factor, 0.0)
            for lag in range(lags):
                part_ref[slot, lag, row] = total[:, lag * chans : (lag + 1) * chans]

    def day_copy(step, slot):
        target = (day + step) % days
        return pltpu.make_async_remote_copy(
            src_ref=part_ref.at[slot, target],
            dst_ref=day_buf.at[step - 1, slot],
            send_sem=day_send.at[step - 1, slot],
            recv_sem=day_recv.at[step - 1, slot],
            device_id={"day": target},
            device_id_type=MESH,
        )

    def day_total(slot):
        total = part_ref[slot, day]
        for step in range(1, days):
            day_copy(step, slot).wait_recv()
            total = total + day_buf[step - 1, slot]
        return total

    def tile_copy(target, source):
        return pltpu.make_async_remote_copy(
            src_ref=send_buf.at[target],
            dst_ref=recv_buf.at[source],
            send_sem=tile_send.at[target],
            recv_sem=tile_recv.at[source],
            device_id={"tile": base + target},
            device_id_type=MESH,
        )

    def top_copy(device, slot):
        return pltpu.make_async_remote_copy(
            src_ref=send_buf.at[group],
            dst_ref=top_buf.at[slot],
            send_sem=top_send,
            recv_sem=top_recv.at[slot],
            device_id={"tile": device},
            device_id_type=MESH,
        )

    def down_copy(row, device):
        return pltpu.make_async_remote_copy(
            src_ref=down_src.at[row],
            dst_ref=down_buf.at[row],
            send_sem=down_send.at[row],
            recv_sem=down_recv.at[row],
            device_id={"tile": device},
            device_id_type=MESH,
        )

    def destination(step):
        is_last = spot // last
        return is_last * step + (1 - is_last) * ((spot + step) % last if step else last)

    def push(step):
        target = destination(step)
        total = day_total(target)

        @pl.when(target == spot)
        def _():
            out_ref[0] = total

        @pl.when(target != spot)
        def _():
            send_buf[target] = total.astype(jnp.bfloat16)
            tile_copy(target, spot).start()

    for turn in range(group):
        target = destination(turn)
        products((target + BELOW) % group, target)
        for step in range(1, days):
            day_copy(step, target).start()
        if turn:
            push(turn - 1)

    @pl.when(is_top)
    def _():
        products(group, group)
        for step in range(1, days):
            day_copy(step, group).start()

    push(last)

    @pl.when(is_top)
    def _():
        total = day_total(group)

        @pl.when(spot < last)
        def _():
            send_buf[group] = total.astype(jnp.bfloat16)
            top_copy(base + last, spot).start()

        @pl.when(spot == last)
        def _():
            part_ref[group, day] = total

    for offset in range(last, 0, -1):
        tile_copy(spot, mixed(spot, offset)).wait_recv()
    sends_down = has_below & (spot == last)
    takes_down = has_above & (spot == last)
    for row in range(rows_dev):
        total = out_ref[0, row]
        for offset in range(last, 0, -1):
            total = total + recv_buf[mixed(spot, offset), row].astype(jnp.float32)
        out_ref[0, row] = total

        @pl.when(sends_down)
        def _():
            down_src[row] = total.astype(jnp.bfloat16)
            down_copy(row, here - group).start()

    @pl.when(takes_down)
    def _():
        for row in range(rows_dev):
            down_copy(row, here).wait_recv()
            out_ref[0, row] = down_buf[row].astype(jnp.float32)

    @pl.when(is_top & (spot == last))
    def _():
        total = part_ref[group, day]
        for slot in range(last):
            top_copy(here, slot).wait_recv()
            total = total + top_buf[slot].astype(jnp.float32)
        out_ref[0] = total

    @pl.when(is_top & (spot < last))
    def _():
        top_copy(base + last, spot).wait_send()

    @pl.when(sends_down)
    def _():
        for row in range(rows_dev):
            down_copy(row, here - group).wait_send()

    for offset in range(last, 0, -1):
        tile_copy(mixed(spot, offset), spot).wait_send()
    for offset in range(last, -1, -1):
        for step in range(1, days):
            day_copy(step, offset).wait_send()

    @pl.when(is_top)
    def _():
        for step in range(1, days):
            day_copy(step, group).wait_send()


def per_device(tiles, days, spectra, band_low, band_high, pair_list):
    own = spectra[0]
    channels, parts, segments, bins = own.shape
    group = segments
    chans = channels // BLK_DEV
    rows_dev = pair_list.shape[0]
    lags = days
    norm_factor = 1.0 / math.sqrt(segments * bins * days)
    slice_shape = (parts, BLK_DEV, chans, bins)
    raw = jnp.transpose(own.reshape(BLK_DEV, chans, parts, segments, bins), (3, 2, 0, 1, 4))

    chunks = 2 * BLK_DEV
    block_shape = (rows_dev, chans, chans)
    gathered_shape = (BELOW + group, 8, 128)
    return pl.pallas_call(
        functools.partial(correlate_kernel, tiles, days, group, norm_factor),
        out_shape=jax.ShapeDtypeStruct((1,) + block_shape, jnp.float32),
        in_specs=[SMEM, SMEM, VMEM, VMEM, pl.BlockSpec(memory_space=pl.ANY)],
        out_specs=VMEM,
        scratch_shapes=[
            pltpu.VMEM((segments,) + slice_shape, jnp.bfloat16),
            pltpu.SemaphoreType.DMA((group, BLK_DEV)),
            pltpu.VMEM((segments,) + slice_shape, jnp.bfloat16),
            pltpu.VMEM((bins, bins), jnp.bfloat16),
            pltpu.VMEM((group + REACH,) + slice_shape, jnp.bfloat16),
            pltpu.VMEM(gathered_shape, jnp.int32),
            pltpu.SMEM(gathered_shape, jnp.int32),
            pltpu.VMEM(((group + REACH) * BLK_DEV, parts, lags * chans, bins), jnp.bfloat16),
            pltpu.VMEM((group + 1, lags) + block_shape, jnp.float32),
            pltpu.VMEM((days - 1, group + 1) + block_shape, jnp.float32),
            pltpu.VMEM((group + 1,) + block_shape, jnp.bfloat16),
            pltpu.VMEM((group,) + block_shape, jnp.bfloat16),
            pltpu.VMEM((group - 1,) + block_shape, jnp.bfloat16),
            pltpu.VMEM(block_shape, jnp.bfloat16),
            pltpu.VMEM(block_shape, jnp.bfloat16),
            pltpu.SemaphoreType.DMA((group - 1, chunks)),
            pltpu.SemaphoreType.DMA((group - 1, chunks)),
            pltpu.SemaphoreType.DMA((REACH, chunks)),
            pltpu.SemaphoreType.DMA((REACH, chunks)),
            pltpu.SemaphoreType.DMA((group - 1,)),
            pltpu.SemaphoreType.DMA((group - 1,)),
            pltpu.SemaphoreType.DMA,
            pltpu.SemaphoreType.DMA,
            pltpu.SemaphoreType.DMA,
            pltpu.SemaphoreType.DMA((days - 1, group + 1)),
            pltpu.SemaphoreType.DMA((days - 1, group + 1)),
            pltpu.SemaphoreType.DMA((group,)),
            pltpu.SemaphoreType.DMA((group,)),
            pltpu.SemaphoreType.DMA,
            pltpu.SemaphoreType.DMA((group - 1,)),
            pltpu.SemaphoreType.DMA((rows_dev,)),
            pltpu.SemaphoreType.DMA((rows_dev,)),
        ],
        compiler_params=pltpu.CompilerParams(
            collective_id=0, has_side_effects=True, vmem_limit_bytes=63 * 1024 * 1024
        ),
    )(band_low, band_high, pair_list.T, jnp.asarray(phase_tables(lags, bins)), raw)


def solution(mesh):
    placed = (P("day", "tile", None, None, None), P("tile"), P("tile"), P("tile", None))
    return jax.shard_map(
        functools.partial(per_device, mesh.shape["tile"], mesh.shape["day"]),
        mesh=mesh,
        in_specs=placed,
        out_specs=P("day", "tile", None, None),
        check_vma=False,
    )
```

profile of v0, /device:TPU:31, one launch (start us, length us, event | category | flops | bytes accessed | tf_op | source)
XLA Modules:
  0.0 54.6 jit_solution(3404615980867184723)
XLA Ops:
  0.0 3.6 %copy.6 = bf16[1,256,2,4,512]{4,1,2,3,0:T(8,128)(2,1)} copy(bf16[1,256,2,4,512]{4,3,2,1,0:T(4,128)(2,1)} %param.5) | data formatting | bytes 4194304 | tf_op args[0]
  3.6 49.3 %shard_map.55 = f32[1,4,128,128]{3,2,1,0:T(8,128)} custom-call(s32[2]{0:T(128)} %low_ref.1, s32[2]{0:T(128)} %high_ref.1, s32[2,4]{1,0:T(2,128)} %bitcast.5, f32[2,2,512]{2,1,0:T(2,128)} %constant.2.clone.trig_ref, bf16[4,2,2,128,512]{4,3,2,1,0:T(8,128)(2,1)} %bitcast.4), custom_call_target="tpu_custom_call" | custom-call | tf_op jit(solution)/shard_map/pallas_call | solution.py:436
  52.9 1.7 %copy.8 = f32[1,4,128,128]{3,2,1,0:T(8,128)} copy(f32[1,4,128,128]{3,2,1,0:T(8,128)} %shard_map.55) | data formatting | bytes 524288
where the time goes:
time: 55.5 us; the launch traced here: 54.6 us
  Pallas kernels  49.3 us (89%)
  local copies, waits for them, and re-layouts  5.27 us (9%)
    pallas_call x1, Pallas kernels, per_device(): pl.pallas_call(functools.partial(correlate_kernel, tiles, days, group, no...  49.3 us
    unnamed x2, local copies, waits for them, and re-layouts  5.27 us

commit v1 on v0

v1 whole, which is shorter than its diff:
```python
import functools
import math

import jax
import jax.numpy as jnp
import numpy as np
from jax import lax
from jax.experimental import pallas as pl
from jax.experimental.pallas import tpu as pltpu
from jax.sharding import PartitionSpec as P

BLK_DEV = 2
SEGLEN = 15000
FIRST = 90
HALF_WIN = 64
LSTEP = 25
REACH = 3
BELOW = 1
MESH = pl.DeviceIdType.MESH
VMEM = pl.BlockSpec(memory_space=pltpu.VMEM)
SMEM = pl.BlockSpec(memory_space=pltpu.SMEM)


def phase_tables(lag_total, bin_count):
    lag_samples = (np.arange(lag_total) - lag_total // 2) * LSTEP
    bin_number = FIRST + np.arange(bin_count)
    phase_turns = lag_samples[:, None] * bin_number[None, :] % SEGLEN
    phase_angle = phase_turns.astype(np.float32) * np.float32(2.0 * math.pi / SEGLEN)
    return np.stack([np.cos(phase_angle), np.sin(phase_angle)], axis=1).astype(np.float32)


def mixed(index, offset):
    result = index
    bit = 1
    while bit <= offset:
        if offset & bit:
            result = result + bit - 2 * bit * ((index // bit) % 2)
        bit *= 2
    return result


LANES = 128
ITEM = 32
EARLY = 2


def message_list(channels, item, quarters):
    early = min(EARLY, quarters)
    messages = [(0, early, start, item) for start in range(0, channels, item)]
    for quarter in range(early, quarters):
        size = item if quarter == quarters - 1 else 2 * item
        messages += [(quarter, 1, start, size) for start in range(0, channels, size)]
    return messages


def correlate_kernel(
    tiles, days, group, norm_factor, messages, low_ref, high_ref, own_pair_ref, trig_ref, raw_hbm, out_ref,
    raw_ref, raw_sem, perm_ref, stage_ref, own_ref, spread_ref, win_ref, gath_ref, pair_ref,
    rot_ref, part_ref, day_buf, send_buf, recv_buf, via_buf, top_buf, down_src, down_buf,
    send_sem, recv_sem, far_send, far_recv, pair_send, pair_recv, up_send, up_recv, own_sem,
    day_send, day_recv, tile_send, tile_recv, via_recv, top_send, top_recv, down_send, down_recv,
):
    here = lax.axis_index("tile")
    day = lax.axis_index("day")
    spot = here % group
    base = here - spot
    has_below = base > 0
    has_above = base + group < tiles
    is_top = base + group == tiles
    upper = REACH - BELOW
    last = group - 1
    base_block = (base - BELOW) * BLK_DEV
    window_tiles, quarters, channels, wide = win_ref.shape
    chans = channels // BLK_DEV
    bins = spread_ref.shape[0]
    lags = days
    zero_lag = lags // 2
    rows_dev = out_ref.shape[1]
    item = stage_ref.shape[1] // group
    items = channels // item
    item_rows = raw_ref.shape[0] // items
    perm_rows = perm_ref.shape[0]

    def fetch(index):
        rows = pl.ds(index * item_rows, item_rows)
        return pltpu.make_async_copy(raw_hbm.at[rows], raw_ref.at[rows], raw_sem.at[index])

    for index in range(items):
        fetch(index).start()

    barrier = pltpu.get_barrier_semaphore()
    for offset in range(1, days):
        pl.semaphore_signal(
            barrier, inc=1, device_id={"day": (day + offset) % days}, device_id_type=MESH
        )
    for offset in range(1, group):
        pl.semaphore_signal(
            barrier, inc=1, device_id={"tile": base + mixed(spot, offset)}, device_id_type=MESH
        )

    @pl.when(has_below)
    def _():
        pl.semaphore_signal(barrier, inc=1, device_id={"tile": here - group}, device_id_type=MESH)

    @pl.when(has_above)
    def _():
        pl.semaphore_signal(barrier, inc=1, device_id={"tile": here + group}, device_id_type=MESH)

    row = lax.broadcasted_iota(jnp.int32, (bins, bins), 0)
    col = lax.broadcasted_iota(jnp.int32, (bins, bins), 1)
    spread_ref[...] = jnp.where(jnp.abs(row - col) <= HALF_WIN, 1.0, 0.0).astype(jnp.bfloat16)
    bin_index = lax.broadcasted_iota(jnp.int32, (1, bins), 1)
    counts = (
        jnp.minimum(bin_index + HALF_WIN, bins - 1) - jnp.maximum(bin_index - HALF_WIN, 0) + 1
    ).astype(jnp.float32)
    inverse_counts = 1.0 / counts

    unit = perm_rows // (2 * quarters * group)
    perm_row = lax.broadcasted_iota(jnp.int32, (perm_rows, perm_rows), 0)
    perm_col = lax.broadcasted_iota(jnp.int32, (perm_rows, perm_rows), 1)
    unit_bits = unit.bit_length() - 1
    quarter_bits = quarters.bit_length() - 1
    group_bits = group.bit_length() - 1
    of_unit = perm_row & (unit - 1)
    of_quarter = (perm_row >> unit_bits) & (quarters - 1)
    of_part = (perm_row >> (unit_bits + quarter_bits)) & 1
    of_segment = perm_row >> (unit_bits + quarter_bits + 1)
    source_row = of_segment + (
        (of_quarter + ((of_part + (of_unit << 1)) << quarter_bits)) << group_bits
    )
    perm_ref[...] = jnp.where(source_row == perm_col, 1.0, 0.0).astype(jnp.bfloat16)

    gath_ref[BELOW + spot, 0:2, 0:rows_dev] = own_pair_ref[...]

    @pl.when(base == 0)
    def _():
        gath_ref[0] = jnp.full(gath_ref.shape[1:], -1, jnp.int32)

    peers = days - 1 + group - 1 + has_below.astype(jnp.int32) + has_above.astype(jnp.int32)
    pl.semaphore_wait(barrier, peers)

    def regroup(index):
        sets = item_rows // perm_rows
        for first in range(0, sets, 2):
            start = index * item_rows + first * perm_rows
            pair = jnp.concatenate(
                [
                    raw_ref[start : start + perm_rows],
                    raw_ref[start + perm_rows : start + 2 * perm_rows],
                ],
                axis=1,
            )
            moved = jnp.dot(perm_ref[...], pair, preferred_element_type=jnp.float32)
            for segment in range(group):
                for part in range(2):
                    for quarter in range(quarters):
                        top = ((segment * 2 + part) * quarters + quarter) * unit
                        for half in range(2):
                            target = segment * item + (first + half) * unit
                            stage_ref[
                                part, target : target + unit, quarter * LANES : (quarter + 1) * LANES
                            ] = moved[top : top + unit, half * LANES : (half + 1) * LANES]

    def whiten(index):
        regroup(index)
        real = stage_ref[0]
        imag = stage_ref[1]
        magnitude = jnp.sqrt(real * real + imag * imag)
        coarse = magnitude.astype(jnp.bfloat16)
        fine = (magnitude - coarse.astype(jnp.float32)).astype(jnp.bfloat16)
        both = jnp.dot(
            jnp.concatenate([coarse, fine], axis=0),
            spread_ref[...],
            preferred_element_type=jnp.float32,
        )
        count = group * item
        amplitude = (both[:count] + both[count:]) * inverse_counts + 1e-05
        block = index * item // chans
        keep = (bin_index >= low_ref[block]) & (bin_index < high_ref[block])
        gain = jnp.where(keep, 1.0 / amplitude, 0.0)
        start = index * item
        for part in range(2):
            white = (stage_ref[part] * gain).astype(jnp.bfloat16)
            for segment in range(group):
                for quarter in range(quarters):
                    own_ref[
                        segment, quarter, start : start + item, part * LANES : (part + 1) * LANES
                    ] = white[
                        segment * item : (segment + 1) * item,
                        quarter * LANES : (quarter + 1) * LANES,
                    ]

    def piece(ref, slot, message):
        quarter, count, start, size = messages[message]
        return ref.at[slot, pl.ds(quarter, count), pl.ds(start, size)]

    def across(offset, message):
        there = mixed(spot, offset)
        return pltpu.make_async_remote_copy(
            src_ref=piece(own_ref, there, message),
            dst_ref=piece(win_ref, BELOW + spot, message),
            send_sem=send_sem.at[offset - 1, message],
            recv_sem=recv_sem.at[offset - 1, message],
            device_id={"tile": base + there},
            device_id_type=MESH,
        )

    def pairs_across(offset):
        return pltpu.make_async_remote_copy(
            src_ref=gath_ref.at[BELOW + spot],
            dst_ref=gath_ref.at[BELOW + spot],
            send_sem=pair_send.at[offset - 1],
            recv_sem=pair_recv.at[offset - 1],
            device_id={"tile": base + mixed(spot, offset)},
            device_id_type=MESH,
        )

    def pairs_up():
        return pltpu.make_async_remote_copy(
            src_ref=gath_ref.at[group],
            dst_ref=gath_ref.at[0],
            send_sem=up_send,
            recv_sem=up_recv,
            device_id={"tile": here + group},
            device_id_type=MESH,
        )

    def far(source, slot, target, device, message):
        index = 0 if target == 0 else target - BELOW - group + 1
        return pltpu.make_async_remote_copy(
            src_ref=piece(source, slot, message),
            dst_ref=piece(win_ref, target, message),
            send_sem=far_send.at[index, message],
            recv_sem=far_recv.at[index, message],
            device_id={"tile": device},
            device_id_type=MESH,
        )

    def relay(source, slot, where, message):
        for lower in range(upper):

            @pl.when(has_below & (where == lower))
            def _():
                far(source, slot, BELOW + group + lower, here - group, message).start()

        @pl.when(has_above & (where == last))
        def _():
            far(source, slot, 0, here + group, message).start()

    def send(message):
        for offset in (last, *range(1, last)):
            across(offset, message).start()
        relay(own_ref, spot, spot, message)

    def arrive(message):
        for offset in range(1, group):
            across(offset, message).wait_recv()
            there = mixed(spot, offset)
            relay(win_ref, BELOW + there, there, message)

    def arrive_below(message_range):
        @pl.when(has_below)
        def _():
            for message in message_range:
                far(own_ref, 0, 0, here, message).wait_recv()

    def arrive_above(message_range):
        @pl.when(has_above)
        def _():
            for message in message_range:
                for lower in range(upper):
                    far(own_ref, 0, BELOW + group + lower, here, message).wait_recv()

    def rotate(source, index, slot, quarter):
        span = slice(quarter * LANES, (quarter + 1) * LANES)
        for block in range(BLK_DEV):
            rows = slice(block * chans, (block + 1) * chans)
            target = slot * BLK_DEV + block
            rot_ref[target, zero_lag * chans : (zero_lag + 1) * chans] = source[index, quarter, rows]
            real = source[index, quarter, rows, 0:LANES].astype(jnp.float32)
            imag = source[index, quarter, rows, LANES:wide].astype(jnp.float32)
            for lag in range(lags):
                if lag == zero_lag:
                    continue
                cosine = trig_ref[lag, 0:1, span]
                sine = trig_ref[lag, 1:2, span]
                out_rows = slice(lag * chans, (lag + 1) * chans)
                rot_ref[target, out_rows, 0:LANES] = (real * cosine + imag * sine).astype(jnp.bfloat16)
                rot_ref[target, out_rows, LANES:wide] = (imag * cosine - real * sine).astype(
                    jnp.bfloat16
                )

    def rotate_near(quarter):
        rotate(own_ref, spot, BELOW + spot, quarter)
        for offset in range(1, group):
            slot = BELOW + mixed(spot, offset)
            rotate(win_ref, slot, slot, quarter)

    def rotate_below(quarter):
        for slot in range(BELOW):
            rotate(win_ref, slot, slot, quarter)

    def rotate_above(quarter):
        for slot in range(BELOW + group, window_tiles):
            rotate(win_ref, slot, slot, quarter)

    def product(set_index, row, quarter):
        first = pair_ref[set_index, 0, row]
        second = pair_ref[set_index, 1, row]
        left = jnp.clip(first - base_block, 0, window_tiles * BLK_DEV - 1)
        right = jnp.clip(second - base_block, 0, window_tiles * BLK_DEV - 1)
        total = lax.dot_general(
            rot_ref[left, zero_lag * chans : (zero_lag + 1) * chans],
            rot_ref[right],
            (((1,), (1,)), ((), ())),
            preferred_element_type=jnp.float32,
        )
        for lag in range(lags):
            value = total[:, lag * chans : (lag + 1) * chans]
            if quarter:
                value = value + part_ref[set_index, lag, row]
            if quarter == quarters - 1:
                value = jnp.where(first >= 0, value * norm_factor, 0.0)
            part_ref[set_index, lag, row] = value

    def compute(quarter):
        rotate_near(quarter)
        rotate_below(quarter)
        rotate_above(quarter)

        def one_set(set_index, carry):
            for row in range(rows_dev):
                product(set_index, row, quarter)
            return carry

        lax.fori_loop(0, group + is_top.astype(jnp.int32), one_set, 0)

    for index in range(items):
        fetch(index).wait()
        whiten(index)
        if index:
            send(index - 1)
        else:
            for peer in range(1, group):
                pairs_across(peer).start()
        if index >= 3:
            arrive(index - 3)
    for message in range(items - 1, len(messages)):
        send(message)
    for index in range(max(items - 3, 0), items):
        arrive(index)
    for offset in range(1, group):
        pairs_across(offset).wait()

    @pl.when(has_above)
    def _():
        pairs_up().start()

    by_quarter = [
        [m for m in range(len(messages)) if messages[m][0] <= q < messages[m][0] + messages[m][1]]
        for q in range(quarters)
    ]
    early = messages[0][1]
    pending = [m for m in range(items, len(messages))]
    final = quarters - 1

    def take(count):
        for _ in range(count):
            if pending:
                arrive(pending.pop(0))

    take(len(by_quarter[early]) if early < final else 0)

    @pl.when(has_above)
    def _():
        pairs_up().wait_send()

    @pl.when(has_below)
    def _():
        pairs_up().wait_recv()

    gather_pairs = pltpu.make_async_copy(gath_ref, pair_ref, own_sem)
    gather_pairs.start()
    arrive_below(by_quarter[0])
    arrive_above(by_quarter[0])
    gather_pairs.wait()
    for quarter in range(final):
        if quarter >= early:
            arrive_below(by_quarter[quarter])
            arrive_above(by_quarter[quarter])
        compute(quarter)
        take(len(pending) if quarter == final - 1 else 2 if quarter == final - 2 else len(pending) // 2)
    rotate_near(final)

    def day_copy(step, slot, row):
        target = (day + step) % days
        return pltpu.make_async_remote_copy(
            src_ref=part_ref.at[slot, target, row],
            dst_ref=day_buf.at[step - 1, slot, row],
            send_sem=day_send.at[step - 1, slot, row],
            recv_sem=day_recv.at[step - 1, slot, row],
            device_id={"day": target},
            device_id_type=MESH,
        )

    def day_total(slot, row):
        total = part_ref[slot, day, row]
        for step in range(1, days):
            day_copy(step, slot, row).wait_recv()
            total = total + day_buf[step - 1, slot, row]
        return total

    def to_via(row):
        return pltpu.make_async_remote_copy(
            src_ref=send_buf.at[2, row],
            dst_ref=via_buf.at[row],
            send_sem=tile_send.at[2, row],
            recv_sem=via_recv.at[row],
            device_id={"tile": base + mixed(spot, 1)},
            device_id_type=MESH,
        )

    def to_owner(kind, row):
        return pltpu.make_async_remote_copy(
            src_ref=send_buf.at[kind, row],
            dst_ref=recv_buf.at[kind, row],
            send_sem=tile_send.at[kind, row],
            recv_sem=tile_recv.at[kind, row],
            device_id={"tile": base + mixed(spot, kind + 1)},
            device_id_type=MESH,
        )

    def top_copy(device, slot, row):
        return pltpu.make_async_remote_copy(
            src_ref=send_buf.at[3, row],
            dst_ref=top_buf.at[slot, row],
            send_sem=top_send.at[row],
            recv_sem=top_recv.at[slot, row],
            device_id={"tile": device},
            device_id_type=MESH,
        )

    def down_copy(row, device):
        return pltpu.make_async_remote_copy(
            src_ref=down_src.at[row],
            dst_ref=down_buf.at[row],
            send_sem=down_send.at[row],
            recv_sem=down_recv.at[row],
            device_id={"tile": device},
            device_id_type=MESH,
        )

    outer = (spot == 0) | (spot == last)
    is_outer = outer.astype(jnp.int32)
    sends_down = has_below & (spot == last)
    takes_down = has_above & (spot == last)

    def set_of(target):
        return (target + BELOW) % group

    def choose(one, other):
        return set_of(is_outer * one + (1 - is_outer) * other)

    first_near = choose(mixed(spot, 3), mixed(spot, 1))
    second_near = choose(spot, mixed(spot, 2))
    first_far = choose(mixed(spot, 1), mixed(spot, 3))
    second_far = choose(mixed(spot, 2), spot)

    def finish(slot):
        for row in range(rows_dev):
            product(slot, row, final)
            for step in range(1, days):
                day_copy(step, slot, row).start()

    def push_first(slot, diagonal):
        for row in range(rows_dev):
            total = day_total(slot, row).astype(jnp.bfloat16)

            @pl.when(diagonal)
            def _():
                send_buf[2, row] = total
                to_via(row).start()

            @pl.when(jnp.logical_not(diagonal))
            def _():
                send_buf[0, row] = total
                to_owner(0, row).start()

    def push_via(slot):
        for row in range(rows_dev):
            total = day_total(slot, row)
            to_via(row).wait_recv()
            send_buf[1, row] = (total + via_buf[row].astype(jnp.float32)).astype(jnp.bfloat16)
            to_owner(1, row).start()

    def settle(slot):
        for row in range(rows_dev):
            total = day_total(slot, row)
            for kind in range(2):
                to_owner(kind, row).wait_recv()
                total = total + recv_buf[kind, row].astype(jnp.float32)
            out_ref[0, row] = total

            @pl.when(sends_down)
            def _():
                down_src[row] = total.astype(jnp.bfloat16)
                down_copy(row, here - group).start()

    finish(set_of(0))
    arrive_below(by_quarter[final])
    rotate_below(final)
    finish(set_of(last))
    push_first(first_near, outer)

    @pl.when(is_top)
    def _():
        finish(group)

    arrive_above(by_quarter[final])
    rotate_above(final)
    finish(first_far)

    @pl.when(jnp.logical_not(outer))
    def _():
        push_via(second_near)

    push_first(first_far, jnp.logical_not(outer))

    @pl.when(is_top & (spot < last))
    def _():
        for row in range(rows_dev):
            send_buf[3, row] = day_total(group, row).astype(jnp.bfloat16)
            top_copy(base + last, spot, row).start()

    finish(second_far)

    @pl.when(outer)
    def _():
        settle(second_near)
        push_via(second_far)

    @pl.when(jnp.logical_not(outer))
    def _():
        settle(second_far)

    @pl.when(is_top & (spot == last))
    def _():
        for row in range(rows_dev):
            total = day_total(group, row)
            for slot in range(last):
                top_copy(here, slot, row).wait_recv()
                total = total + top_buf[slot, row].astype(jnp.float32)
            out_ref[0, row] = total

    @pl.when(is_top & (spot < last))
    def _():
        for row in range(rows_dev):
            top_copy(base + last, spot, row).wait_send()

    @pl.when(takes_down)
    def _():
        for row in range(rows_dev):
            down_copy(row, here).wait_recv()
            out_ref[0, row] = down_buf[row].astype(jnp.float32)

    @pl.when(sends_down)
    def _():
        for row in range(rows_dev):
            down_copy(row, here - group).wait_send()

    for row in range(rows_dev):
        to_via(row).wait_send()
        for kind in range(2):
            to_owner(kind, row).wait_send()
        for step in range(1, days):
            for slot in range(group):
                day_copy(step, slot, row).wait_send()

    @pl.when(is_top)
    def _():
        for row in range(rows_dev):
            for step in range(1, days):
                day_copy(step, group, row).wait_send()

    for message in range(len(messages)):
        for offset in range(1, group):
            across(offset, message).wait_send()

    @pl.when(has_above)
    def _():
        for message in range(len(messages)):
            far(own_ref, 0, 0, here + group, message).wait_send()

    @pl.when(has_below)
    def _():
        for message in range(len(messages)):
            for lower in range(upper):
                far(own_ref, 0, BELOW + group + lower, here - group, message).wait_send()


def per_device(tiles, days, spectra, band_low, band_high, pair_list):
    own = spectra[0]
    channels, parts, segments, bins = own.shape
    group = segments
    chans = channels // BLK_DEV
    rows_dev = pair_list.shape[0]
    lags = days
    norm_factor = 1.0 / math.sqrt(segments * bins * days)
    quarters = bins // LANES
    messages = message_list(channels, ITEM, quarters)
    raw = own.reshape(channels, parts, segments, quarters, LANES)
    raw = jnp.transpose(raw, (0, 1, 3, 2, 4)).reshape(-1, LANES)
    perm_rows = 8 * parts * segments * quarters
    count = len(messages)

    block_shape = (rows_dev, chans, chans)
    gathered_shape = (BELOW + group, 8, 128)
    wide = parts * LANES
    return pl.pallas_call(
        functools.partial(correlate_kernel, tiles, days, group, norm_factor, messages),
        out_shape=jax.ShapeDtypeStruct((1,) + block_shape, jnp.float32),
        in_specs=[SMEM, SMEM, VMEM, VMEM, pl.BlockSpec(memory_space=pl.ANY)],
        out_specs=VMEM,
        scratch_shapes=[
            pltpu.VMEM(raw.shape, jnp.bfloat16),
            pltpu.SemaphoreType.DMA((channels // ITEM,)),
            pltpu.VMEM((perm_rows, perm_rows), jnp.bfloat16),
            pltpu.VMEM((parts, segments * ITEM, bins), jnp.float32),
            pltpu.VMEM((segments, quarters, channels, wide), jnp.bfloat16),
            pltpu.VMEM((bins, bins), jnp.bfloat16),
            pltpu.VMEM((group + REACH, quarters, channels, wide), jnp.bfloat16),
            pltpu.VMEM(gathered_shape, jnp.int32),
            pltpu.SMEM(gathered_shape, jnp.int32),
            pltpu.VMEM(((group + REACH) * BLK_DEV, lags * chans, wide), jnp.bfloat16),
            pltpu.VMEM((group + 1, lags) + block_shape, jnp.float32),
            pltpu.VMEM((days - 1, group + 1) + block_shape, jnp.float32),
            pltpu.VMEM((4,) + block_shape, jnp.bfloat16),
            pltpu.VMEM((2,) + block_shape, jnp.bfloat16),
            pltpu.VMEM(block_shape, jnp.bfloat16),
            pltpu.VMEM((group - 1,) + block_shape, jnp.bfloat16),
            pltpu.VMEM(block_shape, jnp.bfloat16),
            pltpu.VMEM(block_shape, jnp.bfloat16),
            pltpu.SemaphoreType.DMA((group - 1, count)),
            pltpu.SemaphoreType.DMA((group - 1, count)),
            pltpu.SemaphoreType.DMA((REACH, count)),
            pltpu.SemaphoreType.DMA((REACH, count)),
            pltpu.SemaphoreType.DMA((group - 1,)),
            pltpu.SemaphoreType.DMA((group - 1,)),
            pltpu.SemaphoreType.DMA,
            pltpu.SemaphoreType.DMA,
            pltpu.SemaphoreType.DMA,
            pltpu.SemaphoreType.DMA((days - 1, group + 1, rows_dev)),
            pltpu.SemaphoreType.DMA((days - 1, group + 1, rows_dev)),
            pltpu.SemaphoreType.DMA((3, rows_dev)),
            pltpu.SemaphoreType.DMA((2, rows_dev)),
            pltpu.SemaphoreType.DMA((rows_dev,)),
            pltpu.SemaphoreType.DMA((rows_dev,)),
            pltpu.SemaphoreType.DMA((group - 1, rows_dev)),
            pltpu.SemaphoreType.DMA((rows_dev,)),
            pltpu.SemaphoreType.DMA((rows_dev,)),
        ],
        compiler_params=pltpu.CompilerParams(
            collective_id=0, has_side_effects=True, vmem_limit_bytes=63 * 1024 * 1024
        ),
    )(band_low, band_high, pair_list.T, jnp.asarray(phase_tables(lags, bins)), raw)


def solution(mesh):
    placed = (P("day", "tile", None, None, None), P("tile"), P("tile"), P("tile", None))
    return jax.shard_map(
        functools.partial(per_device, mesh.shape["tile"], mesh.shape["day"]),
        mesh=mesh,
        in_specs=placed,
        out_specs=P("day", "tile", None, None),
        check_vma=False,
    )
```

time: 55.5 us -> 52.7 us (0.950)
  local copies, waits for them, and re-layouts: 5.27 us -> 1.67 us
  Pallas kernels: 49.3 us -> 50.6 us
    unnamed x2 -> x1, local copies, waits for them, and re-layouts: 5.27 us -> 1.67 us
    pallas_call x1, Pallas kernels: 49.3 us -> 50.6 us  [per_device(): pl.pallas_call(functools.partial(correlate_kernel, tiles, days, group, no...]
where the time goes in v1:
time: 52.7 us; the launch traced here: 52.3 us
  Pallas kernels  50.6 us (96%)
  local copies, waits for them, and re-layouts  1.67 us (3%)
    pallas_call x1, Pallas kernels, per_device(): pl.pallas_call(functools.partial(correlate_kernel, tiles, days, group, no...  50.6 us
    unnamed x1, local copies, waits for them, and re-layouts  1.67 us

profile of v1, /device:TPU:31, one launch (start us, length us, event | category | flops | bytes accessed | tf_op | source)
XLA Modules:
  0.0 52.3 jit_solution(1479799418603729018)
XLA Ops:
  0.0 50.6 %shard_map.55 = f32[1,4,128,128]{3,2,1,0:T(8,128)} custom-call(s32[2]{0:T(128)} %low_ref.1, s32[2]{0:T(128)} %high_ref.1, s32[2,4]{1,0:T(2,128)} %bitcast.7, f32[2,2,512]{2,1,0:T(2,128)} %constant.2.clone.trig_ref, bf16[8192,128]{1,0:T(8,128)(2,1)} %bitcast.6), custom_call_target="tpu_custom_call" | custom-call | tf_op jit(solution)/shard_map/pallas_call | solution.py:619
  50.6 1.7 %copy.8 = f32[1,4,128,128]{3,2,1,0:T(8,128)} copy(f32[1,4,128,128]{3,2,1,0:T(8,128)} %shard_map.55) | data formatting | bytes 524288

commit v2 on v1

--- a/solution.py
+++ b/solution.py
@@ -40,7 +40,7 @@
 
 
 LANES = 128
-ITEM = 32
+ITEM = 64
 EARLY = 2
 
 
@@ -486,15 +486,15 @@
                 send_buf[0, row] = total
                 to_owner(0, row).start()
 
-    def push_via(slot):
-        for row in range(rows_dev):
+    def push_via(slot, chosen):
+        for row in chosen:
             total = day_total(slot, row)
             to_via(row).wait_recv()
             send_buf[1, row] = (total + via_buf[row].astype(jnp.float32)).astype(jnp.bfloat16)
             to_owner(1, row).start()
 
-    def settle(slot):
-        for row in range(rows_dev):
+    def settle(slot, chosen):
+        for row in chosen:
             total = day_total(slot, row)
             for kind in range(2):
                 to_owner(kind, row).wait_recv()
@@ -520,11 +520,13 @@
     rotate_above(final)
     finish(first_far)
 
+    push_first(first_far, jnp.logical_not(outer))
+
     @pl.when(jnp.logical_not(outer))
     def _():
-        push_via(second_near)
-
-    push_first(first_far, jnp.logical_not(outer))
+        push_via(second_near, range(rows_dev))
+
+    finish(second_far)
 
     @pl.when(is_top & (spot < last))
     def _():
@@ -532,16 +534,15 @@
             send_buf[3, row] = day_total(group, row).astype(jnp.bfloat16)
             top_copy(base + last, spot, row).start()
 
-    finish(second_far)
-
     @pl.when(outer)
     def _():
-        settle(second_near)
-        push_via(second_far)
+        for row in range(rows_dev):
+            settle(second_near, [row])
+            push_via(second_far, [row])
 
     @pl.when(jnp.logical_not(outer))
     def _():
-        settle(second_far)
+        settle(second_far, range(rows_dev))
 
     @pl.when(is_top & (spot == last))
     def _():

time: 52.7 us -> 50.2 us (0.953)
  Pallas kernels: 50.6 us -> 48.3 us
    pallas_call x1, Pallas kernels: 50.6 us -> 48.3 us  [per_device(): pl.pallas_call(functools.partial(correlate_kernel, tiles, days, group, no...]
where the time goes in v2:
time: 50.2 us; the launch traced here: 50 us
  Pallas kernels  48.3 us (96%)
  local copies, waits for them, and re-layouts  1.67 us (3%)
    pallas_call x1, Pallas kernels, per_device(): pl.pallas_call(functools.partial(correlate_kernel, tiles, days, group, no...  48.3 us
    unnamed x1, local copies, waits for them, and re-layouts  1.67 us

profile of v2, /device:TPU:31, one launch (start us, length us, event | category | flops | bytes accessed | tf_op | source)
XLA Modules:
  0.0 50.0 jit_solution(5027176418857113302)
XLA Ops:
  0.0 48.3 %shard_map.55 = f32[1,4,128,128]{3,2,1,0:T(8,128)} custom-call(s32[2]{0:T(128)} %low_ref.1, s32[2]{0:T(128)} %high_ref.1, s32[2,4]{1,0:T(2,128)} %bitcast.7, f32[2,2,512]{2,1,0:T(2,128)} %constant.2.clone.trig_ref, bf16[8192,128]{1,0:T(8,128)(2,1)} %bitcast.6), custom_call_target="tpu_custom_call" | custom-call | tf_op jit(solution)/shard_map/pallas_call | solution.py:620
  48.3 1.7 %copy.8 = f32[1,4,128,128]{3,2,1,0:T(8,128)} copy(f32[1,4,128,128]{3,2,1,0:T(8,128)} %shard_map.55) | data formatting | bytes 524288
